TPU v7x, 256 devices: a whole 4x4x8 slice. The times are simulated.
256 devices in a mesh: rows: 64 (over y_lo, z, x), blk: 4 (over y_hi, core).
Axes of the slice: x: 4, y: 4 (y_hi: 2, y_lo: 2; y = y_hi * 2 + y_lo), z: 8, core: 2. Of those that a mesh axis runs over, the one named last changes fastest.
Arguments:
- block_weight: bfloat16 [64, 4, 4, 64, 128, 128], P('rows', 'blk'), may hold values from 0.049804688 to 50
- block_row: int32 [64, 4, 4, 64], P('rows', 'blk'), may hold values from 0 to 15, as said below
- block_col: int32 [64, 4, 4, 64], P('rows', 'blk'), may hold values from 0 to 7, as said below
- block_count: int32 [64, 4, 4], P('rows', 'blk'), may hold values from 1 to 64, as said below
- block_samples: int32 [64, 4, 4, 64], P('rows', 'blk'), may hold values from 1 to 8
- row_degree: float32 [64, 4, 2048], P('rows', 'blk'), may hold values from 0.125 to 8
- col_degree: float32 [4, 1024], P('blk', 'rows'), may hold values from 1 to 8
- test_matrix: bfloat16 [4, 1024, 128], P('blk', 'rows'), may hold values from -6 to 6
Outputs:
- basis: float32 [64, 4, 2048, 128], P('rows', 'blk')
- triangle: float32 [128, 128], replicated
Inputs may be any that keep to these rules, and one draw needn't show every extreme that they name: Within one band and slab, the slots k < 64 hold distinct (block_row, block_col) pairs. `block_col`: see block_row: pairs are distinct within one band and slab. `block_count`: some band and slab has all 64 slots live in every draw.
All inputs are finite; a program needn't handle non-finite values.
Results may differ from a plain program's by a relative error of at most 0.0065.
Values may be sent and summed in bfloat16 or wider, within the bound.
A program may use at most 64 MiB of HBM per device.

v0:
```python
import jax
import jax.numpy as jnp
from jax import lax
from jax.sharding import PartitionSpec as P

scale_factor = 16.0


def passed_along(block, axis, distance):
    devices = range(lax.axis_size(axis))
    route = [((i - distance) % len(devices), i) for i in devices]
    return lax.ppermute(block, axis, route)


def tile_update(
    running, weights, rows_idx, cols_idx, live_count, samples, row_deg, slab_rows, slab_deg
):
    block_edge = weights.shape[-1]
    capacity = weights.shape[0]
    band_blocks = running.shape[0]
    slab_blocks = slab_rows.shape[0] // block_edge
    slab_tiles = slab_rows.reshape(slab_blocks, block_edge, slab_rows.shape[1])
    picked = slab_tiles[cols_idx]
    col_d = slab_deg.reshape(slab_blocks, block_edge)[cols_idx]
    row_d = row_deg.reshape(band_blocks, block_edge)[rows_idx]
    scaled_ratio = (
        scale_factor
        * weights.astype(jnp.float32)
        / (samples.astype(jnp.float32)[:, None, None] * row_d[:, :, None] * col_d[:, None, :])
    )
    entries = jnp.log(jnp.maximum(scaled_ratio, 1.0)).astype(jnp.bfloat16)
    products = jnp.einsum("kij,kjc->kic", entries, picked, preferred_element_type=jnp.float32)
    alive_mask = (jnp.arange(capacity, dtype=jnp.int32) < live_count).astype(jnp.float32)
    chooser = (rows_idx[None, :] == jnp.arange(band_blocks, dtype=jnp.int32)[:, None]).astype(
        jnp.float32
    ) * alive_mask[None, :]
    return running + jnp.einsum("rk,kic->ric", chooser, products, precision=lax.Precision.HIGHEST)


def body(
    block_weight,
    block_row,
    block_col,
    block_count,
    block_samples,
    row_degree,
    col_degree,
    test_matrix,
):
    loop_size = lax.axis_size("blk")
    position = lax.axis_index("blk")
    weights_all = block_weight[0, 0]
    rows_all = block_row[0, 0]
    cols_all = block_col[0, 0]
    counts_all = block_count[0, 0]
    samples_all = block_samples[0, 0]
    row_deg = row_degree[0, 0]
    block_edge = weights_all.shape[-1]
    band_blocks = row_deg.shape[0] // block_edge
    running = jnp.zeros((band_blocks, block_edge, test_matrix.shape[2]), jnp.float32)
    piece_pair = (test_matrix, col_degree)
    for t in range(loop_size):
        if t > 0:
            piece_pair = (
                passed_along(piece_pair[0], "blk", 1),
                passed_along(piece_pair[1].astype(jnp.bfloat16), "blk", 1).astype(jnp.float32),
            )
        slab_rows, slab_deg = (
            lax.all_gather(piece_pair[0], "rows", axis=1, tiled=True),
            lax.all_gather(piece_pair[1].astype(jnp.bfloat16), "rows", axis=1, tiled=True).astype(
                jnp.float32
            ),
        )
        slab_index = (position - t) % loop_size
        apply_slab_rows = slab_rows[0]
        apply_slab_deg = slab_deg[0]
        slab_index = jnp.asarray(slab_index)
        running = tile_update(
            running,
            lax.dynamic_index_in_dim(weights_all, slab_index, 0, keepdims=False),
            lax.dynamic_index_in_dim(rows_all, slab_index, 0, keepdims=False),
            lax.dynamic_index_in_dim(cols_all, slab_index, 0, keepdims=False),
            lax.dynamic_index_in_dim(counts_all, slab_index, 0, keepdims=False),
            lax.dynamic_index_in_dim(samples_all, slab_index, 0, keepdims=False),
            row_deg,
            apply_slab_rows,
            apply_slab_deg,
        )
    flat_rows = running.reshape(band_blocks * block_edge, running.shape[2])
    gram_local = jnp.dot(
        flat_rows.T, flat_rows, precision=lax.Precision.HIGHEST, preferred_element_type=jnp.float32
    )
    gram_total = lax.psum(gram_local, ("rows", "blk"))
    lower_factor = jnp.linalg.cholesky(gram_total)
    total_rows = flat_rows.shape[0] * lax.axis_size("rows") * loop_size
    root = jnp.sqrt(jnp.float32(total_rows))
    basis_rows = (
        lax.linalg.triangular_solve(
            lower_factor, flat_rows, left_side=False, lower=True, transpose_a=True
        )
        * root
    )
    return (basis_rows.reshape(1, 1, flat_rows.shape[0], flat_rows.shape[1]), lower_factor.T / root)


def solution(mesh):
    placed = (
        P("rows", "blk", None, None, None, None),
        P("rows", "blk", None, None),
        P("rows", "blk", None, None),
        P("rows", "blk", None),
        P("rows", "blk", None, None),
        P("rows", "blk", None),
        P("blk", "rows"),
        P("blk", "rows", None),
    )
    return jax.shard_map(
        body,
        mesh=mesh,
        in_specs=placed,
        out_specs=(P("rows", "blk", None, None), P()),
        check_vma=False,
    )
```

profile of v0, /device:TPU:1, one launch (start us, length us, event | category | flops | bytes accessed | tf_op | source)
XLA Modules:
  0.0 1118.6 jit_solution(2050559915229179514)
XLA Ops:
  7.2 4.4 collective-permute-start.1
  12.3 132.2 %all_gather.25 = bf16[1,1024,128]{2,1,0:T(8,128)(2,1)S(1)} all-gather(bf16[1,16,128]{2,1,0:T(8,128)(2,1)} %param.15), channel_id=1, replica_groups=mesh['rows'=64,'blk'=4] {'rows'}, dimensions={1}, use_global_device_ids=true | all-gather | bytes 266240 | tf_op jit(solution)/shard_map/all_gather | solution.py:69
  158.6 29.4 %collective-permute-start.2 = (bf16[1,16]{1,0:T(2,128)(2,1)S(1)}, bf16[1,16]{1,0:T(2,128)(2,1)S(1)}, u32[]{:S(2)}, u32[]{:S(2)}) collective-permute-start(bf16[1,16]{1,0:T(2,128)(2,1)S(1)} %collective-permute-done), channel_id=1, source_target_pairs={{3,0},{0,1},{1,2},{2,3},{7,4},{4,5},{5,6},{6,7},{11,8},{8,9},{9,10... | collective-permute-start | bytes 104 | tf_op jit(solution)/shard_map/ppermute | solution.py:12
  188.9 3.8 collective-permute-start.4
  193.6 127.1 %all-reduce.4 = (bf16[1024]{0:T(1024)(128)(2,1)S(1)}, bf16[1024]{0:T(1024)(128)(2,1)S(1)}, bf16[1024]{0:T(1024)(128)(2,1)S(1)}, bf16[1024]{0:T(1024)(128)(2,1)S(1)}) all-reduce(bf16[1024]{0:T(1024)(128)(2,1)S(1)} %dynamic-update-slice.4, bf16[1024]{0:T(1024)(128)(2,1)S(1)} %dynamic-update-slice.3, ...), channel_id=1, replica_groups=mesh['rows'=64,'blk'=4] {'rows'}, use_global_device_ids=true, to_apply=%add.1 | all-reduce | flops 4096 | bytes 16384
  321.4 4.1 fusion.21
  327.3 124.8 %all_gather.27 = bf16[1,1024,128]{2,1,0:T(8,128)(2,1)S(1)} all-gather(bf16[1,16,128]{2,1,0:T(8,128)(2,1)S(1)} %collective-permute-done.1), channel_id=1, replica_groups=mesh['rows'=64,'blk'=4] {'rows'}, dimensions={1}, use_global_device_ids=true | all-gather | bytes 266240 | tf_op jit(solution)/shard_map/all_gather | solution.py:69
  453.1 3.6 fusion.23
  456.7 4.4 fusion.16
  461.0 60.1 %collective-permute-start.3 = (bf16[1,16,128]{2,1,0:T(8,128)(2,1)S(1)}, bf16[1,16,128]{2,1,0:T(8,128)(2,1)S(1)}, u32[]{:S(2)}, u32[]{:S(2)}) collective-permute-start(bf16[1,16,128]{2,1,0:T(8,128)(2,1)S(1)} %collective-permute-done.1), channel_id=1, source_target_pairs={{3,0},{0,1},{1,2},{2,3},{7,4},{4,5},{5,6},{6,7},{11,8},{8,9},{9,10... | collective-permute-start | bytes 12296 | tf_op jit(solution)/shard_map/ppermute | solution.py:12
  521.1 4.4 fusion.49
  525.5 124.0 %all_gather.29 = bf16[1,1024,128]{2,1,0:T(8,128)(2,1)S(1)} all-gather(bf16[1,16,128]{2,1,0:T(8,128)(2,1)S(1)} %collective-permute-done.3), channel_id=1, replica_groups=mesh['rows'=64,'blk'=4] {'rows'}, dimensions={1}, use_global_device_ids=true | all-gather | bytes 266240 | tf_op jit(solution)/shard_map/all_gather | solution.py:69
  650.6 3.6 fusion.25
  654.2 27.5 %collective-permute-start.5 = (bf16[1,16,128]{2,1,0:T(8,128)(2,1)S(1)}, bf16[1,16,128]{2,1,0:T(8,128)(2,1)S(1)}, u32[]{:S(2)}, u32[]{:S(2)}) collective-permute-start(bf16[1,16,128]{2,1,0:T(8,128)(2,1)S(1)} %copy-done.3), channel_id=1, source_target_pairs={{3,0},{0,1},{1,2},{2,3},{7,4},{4,5},{5,6},{6,7},{11,8},{8,9},{9,10... | collective-permute-start | bytes 12296 | tf_op jit(solution)/shard_map/ppermute | solution.py:12
  681.8 4.4 fusion.52
  686.2 125.7 %all_gather.31 = bf16[1,1024,128]{2,1,0:T(8,128)(2,1)S(1)} all-gather(bf16[1,16,128]{2,1,0:T(8,128)(2,1)S(1)} %collective-permute-done.5), channel_id=1, replica_groups=mesh['rows'=64,'blk'=4] {'rows'}, dimensions={1}, use_global_device_ids=true | all-gather | bytes 266240 | tf_op jit(solution)/shard_map/all_gather | solution.py:69
  811.9 2.1 gather_fusion.11
  814.0 3.3 fusion.27
  817.4 4.4 fusion.55
  821.8 2.5 convolution_bitcast_fusion
  824.7 259.5 %all-reduce.7.cloned.1.call-done = f32[128,128]{0,1:T(8,128)} async-done(((f32[128,128]{0,1:T(8,128)}), f32[128,128]{0,1:T(8,128)}) %all-reduce.7.cloned.1.call-update) | async-done | bytes 65552 | tf_op jit(solution)/shard_map/psum | solution.py:93
  1086.0 11.7 %cholesky.16 = f32[128,128]{1,0:T(8,128)S(1)} custom-call(f32[128,128]{1,0:T(8,128)S(1)} %fusion.59), custom_call_target="Cholesky" | custom-call | tf_op jit(solution)/shard_map/jit(cholesky)/cholesky | solution.py:94
  1099.1 9.8 custom-call.6
  1109.6 1.9 fusion.20
  (77 shorter events, 24.5 us)
Async XLA Ops:
  7.2 142.5 %copy-start = (f32[1,1,2048]{2,1,0:T(1,128)S(1)}, f32[1,1,2048]{2,1,0:T(1,128)}, u32[]{:S(2)}) copy-start(f32[1,1,2048]{2,1,0:T(1,128)} %param.13) | copy-start | bytes 24580
  7.2 1077.0 %all-reduce.7.cloned.1.call-start = ((), (), s32[]{:S(2)}) async-start(), calls=%async_computation | async-start | bytes 131072 | tf_op jit(solution)/shard_map/psum | solution.py:93
  7.2 320.1 %collective-permute-start.1 = (bf16[1,16,128]{2,1,0:T(8,128)(2,1)}, bf16[1,16,128]{2,1,0:T(8,128)(2,1)S(1)}, u32[]{:S(2)}, u32[]{:S(2)}) collective-permute-start(bf16[1,16,128]{2,1,0:T(8,128)(2,1)} %param.15), channel_id=1, source_target_pairs={{3,0},{0,1},{1,2},{2,3},{7,4},{4,5},{5,6},{6,7},{11,8},{8,9},{9,10... | collective-permute-start | bytes 12296 | tf_op jit(solution)/shard_map/ppermute | solution.py:12
  12.3 146.1 %collective-permute-start = (bf16[1,16]{1,0:T(2,128)(2,1)S(1)}, bf16[1,16]{1,0:T(2,128)(2,1)S(1)}, u32[]{:S(2)}, u32[]{:S(2)}) collective-permute-start(bf16[1,16]{1,0:T(2,128)(2,1)S(1)} %get-tuple-element.33), channel_id=1, source_target_pairs={{3,0},{0,1},{1,2},{2,3},{7,4},{4,5},{5,6},{6,7},{11,8},{8,9},{9,10... | collective-permute-start | bytes 104 | tf_op jit(solution)/shard_map/ppermute | solution.py:12
  158.6 30.1 %collective-permute-start.2 = (bf16[1,16]{1,0:T(2,128)(2,1)S(1)}, bf16[1,16]{1,0:T(2,128)(2,1)S(1)}, u32[]{:S(2)}, u32[]{:S(2)}) collective-permute-start(bf16[1,16]{1,0:T(2,128)(2,1)S(1)} %collective-permute-done), channel_id=1, source_target_pairs={{3,0},{0,1},{1,2},{2,3},{7,4},{4,5},{5,6},{6,7},{11,8},{8,9},{9,10... | collective-permute-start | bytes 104 | tf_op jit(solution)/shard_map/ppermute | solution.py:12
  188.9 4.5 collective-permute-start.4
  456.7 64.4 %copy-start.1 = (f32[64,128,128]{2,1,0:T(8,128)S(1)}, f32[64,128,128]{2,1,0:T(8,128)}, u32[]{:S(2)}) copy-start(f32[64,128,128]{2,1,0:T(8,128)} %fusion.21) | copy-start | bytes 12582916
  461.0 64.5 %collective-permute-start.3 = (bf16[1,16,128]{2,1,0:T(8,128)(2,1)S(1)}, bf16[1,16,128]{2,1,0:T(8,128)(2,1)S(1)}, u32[]{:S(2)}, u32[]{:S(2)}) collective-permute-start(bf16[1,16,128]{2,1,0:T(8,128)(2,1)S(1)} %collective-permute-done.1), channel_id=1, source_target_pairs={{3,0},{0,1},{1,2},{2,3},{7,4},{4,5},{5,6},{6,7},{11,8},{8,9},{9,10... | collective-permute-start | bytes 12296 | tf_op jit(solution)/shard_map/ppermute | solution.py:12
  525.5 124.0 %copy-start.2 = (bf16[1,16,128]{2,1,0:T(8,128)(2,1)}, bf16[1,16,128]{2,1,0:T(8,128)(2,1)S(1)}, u32[]{:S(2)}) copy-start(bf16[1,16,128]{2,1,0:T(8,128)(2,1)S(1)} %collective-permute-done.3) | copy-start | bytes 12292
  650.5 3.7 copy-start.3
  650.5 31.2 %copy-start.5 = (s32[64]{0:T(128)S(1)}, s32[64]{0:T(128)}, u32[]{:S(2)}) copy-start(s32[64]{0:T(128)} %get-tuple-element.15) | copy-start | bytes 772
  650.5 31.2 %copy-start.7 = (f32[64]{0:T(128)S(1)}, f32[64]{0:T(128)}, u32[]{:S(2)}) copy-start(f32[64]{0:T(128)} %compare_convert_fusion.1) | copy-start | bytes 772
  654.2 32.0 %collective-permute-start.5 = (bf16[1,16,128]{2,1,0:T(8,128)(2,1)S(1)}, bf16[1,16,128]{2,1,0:T(8,128)(2,1)S(1)}, u32[]{:S(2)}, u32[]{:S(2)}) collective-permute-start(bf16[1,16,128]{2,1,0:T(8,128)(2,1)S(1)} %copy-done.3), channel_id=1, source_target_pairs={{3,0},{0,1},{1,2},{2,3},{7,4},{4,5},{5,6},{6,7},{11,8},{8,9},{9,10... | collective-permute-start | bytes 12296 | tf_op jit(solution)/shard_map/ppermute | solution.py:12
  814.0 3.4 copy-start.4
  814.0 3.4 copy-start.6
Sparse Core Ops, SparseCore 0:
  824.5 259.6 all-reduce.6
where the time goes:
time: 1120 us
  blocking collectives  634 us (57%)
  waiting for transfers between devices  261 us (23%)
  starting transfers between devices  125 us (11%)
  matrix products  36.7 us (3%)
  other arithmetic  29.9 us (3%)
  local copies, waits for them, and re-layouts  16.8 us (2%)
  between operations  15.2 us (1%)
    all_gather x4, blocking collectives, body(): lax.all_gather(piece_pair[0], 'rows', axis=1, tiled=True)  507 us
    psum x1, waiting for transfers between devices, body(): gram_total = lax.psum(gram_local, ('rows', 'blk'))  260 us
    unnamed x1, blocking collectives  127 us
    ppermute x6, starting transfers between devices, passed_along(): return lax.ppermute(block, axis, route)  125 us
  transfers between devices with their start and end apart: 7, of which 3 were waited for; matrix products, arithmetic and copies ran while one was open for 3% of the time, Pallas kernels for 0%

commit v1 on v0

--- a/solution.py
+++ b/solution.py
@@ -66,7 +66,10 @@
                 passed_along(piece_pair[1].astype(jnp.bfloat16), "blk", 1).astype(jnp.float32),
             )
         slab_rows, slab_deg = (
-            lax.all_gather(piece_pair[0], "rows", axis=1, tiled=True),
+            jnp.concatenate(
+                lax.all_to_all(jnp.stack([piece_pair[0]] * lax.axis_size("rows")), "rows", 0, 0),
+                axis=1,
+            ),
             lax.all_gather(piece_pair[1].astype(jnp.bfloat16), "rows", axis=1, tiled=True).astype(
                 jnp.float32
             ),

time: 1120 us -> 582 us (0.52)
  blocking collectives: 634 us -> 132 us
  starting transfers between devices: 125 us -> 88.7 us
    all_gather x4 -> x0, blocking collectives: 507 us -> none  [body(): lax.all_gather(piece_pair[0], 'rows', axis=1, tiled=True)]
    ppermute x6, starting transfers between devices: 125 us -> 44.7 us  [passed_along(): return lax.ppermute(block, axis, route)]
    all_to_all x0 -> x4, starting transfers between devices: none -> 43.9 us  [body(): lax.all_to_all(jnp.stack([piece_pair[0]] * lax.axis_size('rows')), 'rows'...]
    psum x1, waiting for transfers between devices: 260 us -> 241 us  [body(): gram_total = lax.psum(gram_local, ('rows', 'blk'))]
  transfers between devices with their start and end apart: 7 -> 11, of which waited for: 3 -> 5; matrix products, arithmetic and copies ran while one was open for 3% -> 8% of each run, Pallas kernels for 0% -> 0%
where the time goes in v1:
time: 582 us; the launch traced here: 573 us
  waiting for transfers between devices  251 us (43%)
  blocking collectives  132 us (23%)
  starting transfers between devices  88.7 us (15%)
  matrix products  36.2 us (6%)
  other arithmetic  29 us (5%)
  local copies, waits for them, and re-layouts  21 us (4%)
  between operations  15.5 us (3%)
    psum x1, waiting for transfers between devices, body(): gram_total = lax.psum(gram_local, ('rows', 'blk'))  241 us
    unnamed x1, blocking collectives  132 us
    ppermute x6, starting transfers between devices, passed_along(): return lax.ppermute(block, axis, route)  44.7 us
    all_to_all x4, starting transfers between devices, body(): lax.all_to_all(jnp.stack([piece_pair[0]] * lax.axis_size('rows')), 'rows'...  43.9 us
    dot_general x4, matrix products, tile_update(): jnp.einsum('rk,kic->ric', chooser, products, precision=lax.Precision.HIGH...  17.6 us
    dot_general x4, matrix products, tile_update(): jnp.einsum('kij,kjc->kic', entries, picked, preferred_element_type=jnp.fl...  14.2 us
    another operation x3, other arithmetic, body(): lower_factor = jnp.linalg.cholesky(gram_total)  12.4 us
  transfers between devices with their start and end apart: 11, of which 5 were waited for; matrix products, arithmetic and copies ran while one was open for 8% of the time, Pallas kernels for 0%

profile of v1, /device:TPU:1, one launch (start us, length us, event | category | flops | bytes accessed | tf_op | source)
XLA Modules:
  0.0 573.5 jit_solution(11685440756327927550)
XLA Ops:
  7.2 4.4 collective-permute-start.1
  13.6 11.8 %all-to-all-start = ((bf16[64,1,16,128]{3,2,1,0:T(8,128)(2,1)}), bf16[64,1,16,128]{3,2,1,0:T(8,128)(2,1)S(1)}, u32[]{:S(2)}, u32[]{:S(2)}) async-start(bf16[64,1,16,128]{3,2,1,0:T(8,128)(2,1)} %stack.8), calls=%async_computation | async-start | bytes 524288 | tf_op jit(solution)/shard_map/all_to_all | solution.py:70
  37.3 2.3 collective-permute-start.2
  40.4 3.8 collective-permute-start.4
  45.2 132.3 %all-reduce.4 = (bf16[1024]{0:T(1024)(128)(2,1)S(1)}, bf16[1024]{0:T(1024)(128)(2,1)S(1)}, bf16[1024]{0:T(1024)(128)(2,1)S(1)}, bf16[1024]{0:T(1024)(128)(2,1)S(1)}) all-reduce(bf16[1024]{0:T(1024)(128)(2,1)S(1)} %dynamic-update-slice.4, bf16[1024]{0:T(1024)(128)(2,1)S(1)} %dynamic-update-slice.3, ...), channel_id=1, replica_groups=mesh['rows'=64,'blk'=4] {'rows'}, use_global_device_ids=true, to_apply=%add.1 | all-reduce | flops 4096 | bytes 16384
  177.5 32.1 %collective-permute-start.3 = (bf16[1,16,128]{2,1,0:T(8,128)(2,1)S(1)}, bf16[1,16,128]{2,1,0:T(8,128)(2,1)S(1)}, u32[]{:S(2)}, u32[]{:S(2)}) collective-permute-start(bf16[1,16,128]{2,1,0:T(8,128)(2,1)S(1)} %collective-permute-done.1), channel_id=1, source_target_pairs={{3,0},{0,1},{1,2},{2,3},{7,4},{4,5},{5,6},{6,7},{11,8},{8,9},{9,10... | collective-permute-start | bytes 12296 | tf_op jit(solution)/shard_map/ppermute | solution.py:12
  214.9 4.6 all-to-all-start.1
  220.5 4.1 fusion.21
  224.6 7.4 %all-to-all-done.1 = bf16[64,1,16,128]{3,2,1,0:T(8,128)(2,1)S(1)} async-done(((bf16[64,1,16,128]{3,2,1,0:T(8,128)(2,1)}), bf16[64,1,16,128]{3,2,1,0:T(8,128)(2,1)S(1)}, u32[]{:S(2)}, u32[]{:S(2)}) %all-to-all-start.1) | async-done | bytes 262176 | tf_op jit(solution)/shard_map/all_to_all | solution.py:70
  232.8 16.9 %all-to-all-start.2 = ((bf16[64,1,16,128]{3,2,1,0:T(8,128)(2,1)}), bf16[64,1,16,128]{3,2,1,0:T(8,128)(2,1)S(1)}, u32[]{:S(2)}, u32[]{:S(2)}) async-start(bf16[64,1,16,128]{3,2,1,0:T(8,128)(2,1)} %stack.10), calls=%async_computation.2 | async-start | bytes 524288 | tf_op jit(solution)/shard_map/all_to_all | solution.py:70
  250.6 3.6 fusion.23
  254.2 4.4 fusion.16
  258.6 4.4 fusion.49
  263.8 10.6 %all-to-all-start.3 = ((bf16[64,1,16,128]{3,2,1,0:T(8,128)(2,1)}), bf16[64,1,16,128]{3,2,1,0:T(8,128)(2,1)S(1)}, u32[]{:S(2)}, u32[]{:S(2)}) async-start(bf16[64,1,16,128]{3,2,1,0:T(8,128)(2,1)} %stack.11), calls=%async_computation.3 | async-start | bytes 524288 | tf_op jit(solution)/shard_map/all_to_all | solution.py:70
  274.5 2.2 gather_fusion.8
  276.6 3.1 fusion.25
  279.8 4.4 fusion.52
  285.3 2.2 gather_fusion.11
  287.5 3.3 fusion.27
  290.8 4.4 fusion.55
  295.2 2.5 convolution_bitcast_fusion
  298.1 240.8 %all-reduce.7.cloned.1.call-done = f32[128,128]{0,1:T(8,128)} async-done(((f32[128,128]{0,1:T(8,128)}), f32[128,128]{0,1:T(8,128)}) %all-reduce.7.cloned.1.call-update) | async-done | bytes 65552 | tf_op jit(solution)/shard_map/psum | solution.py:96
  540.7 11.7 %cholesky.16 = f32[128,128]{1,0:T(8,128)S(1)} custom-call(f32[128,128]{1,0:T(8,128)S(1)} %fusion.59), custom_call_target="Cholesky" | custom-call | tf_op jit(solution)/shard_map/jit(cholesky)/cholesky | solution.py:97
  553.7 9.8 %custom-call.6 = f32[1,128,128]{1,2,0:T(8,128)S(1)} custom-call(f32[1,128,128]{2,1,0:T(8,128)S(1)} %get-tuple-element.11), custom_call_target="InvertDiagBlocksLowerTriangular" | custom-call | tf_op jit(solution)/shard_map/triangular_solve | solution.py:101
  (73 shorter events, 30.9 us)
Async XLA Ops:
  7.2 23.0 %copy-start = (f32[1,1,2048]{2,1,0:T(1,128)S(1)}, f32[1,1,2048]{2,1,0:T(1,128)}, u32[]{:S(2)}) copy-start(f32[1,1,2048]{2,1,0:T(1,128)} %param.13) | copy-start | bytes 24580
  7.2 170.3 %collective-permute-start.1 = (bf16[1,16,128]{2,1,0:T(8,128)(2,1)}, bf16[1,16,128]{2,1,0:T(8,128)(2,1)S(1)}, u32[]{:S(2)}, u32[]{:S(2)}) collective-permute-start(bf16[1,16,128]{2,1,0:T(8,128)(2,1)} %param.15), channel_id=1, source_target_pairs={{3,0},{0,1},{1,2},{2,3},{7,4},{4,5},{5,6},{6,7},{11,8},{8,9},{9,10... | collective-permute-start | bytes 12296 | tf_op jit(solution)/shard_map/ppermute | solution.py:12
  12.2 24.8 %collective-permute-start = (bf16[1,16]{1,0:T(2,128)(2,1)S(1)}, bf16[1,16]{1,0:T(2,128)(2,1)S(1)}, u32[]{:S(2)}, u32[]{:S(2)}) collective-permute-start(bf16[1,16]{1,0:T(2,128)(2,1)S(1)} %get-tuple-element.33), channel_id=1, source_target_pairs={{3,0},{0,1},{1,2},{2,3},{7,4},{4,5},{5,6},{6,7},{11,8},{8,9},{9,10... | collective-permute-start | bytes 104 | tf_op jit(solution)/shard_map/ppermute | solution.py:12
  13.6 200.5 %all-to-all-start = ((bf16[64,1,16,128]{3,2,1,0:T(8,128)(2,1)}), bf16[64,1,16,128]{3,2,1,0:T(8,128)(2,1)S(1)}, u32[]{:S(2)}, u32[]{:S(2)}) async-start(bf16[64,1,16,128]{3,2,1,0:T(8,128)(2,1)} %stack.8), calls=%async_computation | async-start | bytes 524288 | tf_op jit(solution)/shard_map/all_to_all | solution.py:70
  37.3 3.0 collective-permute-start.2
  40.4 4.5 collective-permute-start.4
  177.5 34.5 %collective-permute-start.3 = (bf16[1,16,128]{2,1,0:T(8,128)(2,1)S(1)}, bf16[1,16,128]{2,1,0:T(8,128)(2,1)S(1)}, u32[]{:S(2)}, u32[]{:S(2)}) collective-permute-start(bf16[1,16,128]{2,1,0:T(8,128)(2,1)S(1)} %collective-permute-done.1), channel_id=1, source_target_pairs={{3,0},{0,1},{1,2},{2,3},{7,4},{4,5},{5,6},{6,7},{11,8},{8,9},{9,10... | collective-permute-start | bytes 12296 | tf_op jit(solution)/shard_map/ppermute | solution.py:12
  212.0 51.0 %collective-permute-start.5 = (bf16[1,16,128]{2,1,0:T(8,128)(2,1)S(1)}, bf16[1,16,128]{2,1,0:T(8,128)(2,1)S(1)}, u32[]{:S(2)}, u32[]{:S(2)}) collective-permute-start(bf16[1,16,128]{2,1,0:T(8,128)(2,1)S(1)} %collective-permute-done.3), channel_id=1, source_target_pairs={{3,0},{0,1},{1,2},{2,3},{7,4},{4,5},{5,6},{6,7},{11,8},{8,9},{9,10... | collective-permute-start | bytes 12296 | tf_op jit(solution)/shard_map/ppermute | solution.py:12
  214.9 17.1 %all-to-all-start.1 = ((bf16[64,1,16,128]{3,2,1,0:T(8,128)(2,1)}), bf16[64,1,16,128]{3,2,1,0:T(8,128)(2,1)S(1)}, u32[]{:S(2)}, u32[]{:S(2)}) async-start(bf16[64,1,16,128]{3,2,1,0:T(8,128)(2,1)} %stack.9), calls=%async_computation.1 | async-start | bytes 524288 | tf_op jit(solution)/shard_map/all_to_all | solution.py:70
  232.8 30.3 %all-to-all-start.2 = ((bf16[64,1,16,128]{3,2,1,0:T(8,128)(2,1)}), bf16[64,1,16,128]{3,2,1,0:T(8,128)(2,1)S(1)}, u32[]{:S(2)}, u32[]{:S(2)}) async-start(bf16[64,1,16,128]{3,2,1,0:T(8,128)(2,1)} %stack.10), calls=%async_computation.2 | async-start | bytes 524288 | tf_op jit(solution)/shard_map/all_to_all | solution.py:70
  254.2 4.4 copy-start.1
  263.8 21.5 %all-to-all-start.3 = ((bf16[64,1,16,128]{3,2,1,0:T(8,128)(2,1)}), bf16[64,1,16,128]{3,2,1,0:T(8,128)(2,1)S(1)}, u32[]{:S(2)}, u32[]{:S(2)}) async-start(bf16[64,1,16,128]{3,2,1,0:T(8,128)(2,1)} %stack.11), calls=%async_computation.3 | async-start | bytes 524288 | tf_op jit(solution)/shard_map/all_to_all | solution.py:70
  274.4 264.5 %all-reduce.7.cloned.1.call-start = ((), (), s32[]{:S(2)}) async-start(), calls=%async_computation.4 | async-start | bytes 131072 | tf_op jit(solution)/shard_map/psum | solution.py:96
Sparse Core Ops, SparseCore 0:
  297.8 241.0 all-reduce.6
